TPU v7x, 256 devices: a whole 4x4x8 slice. The times are simulated.
256 devices in a mesh: row: 32 (over z, x_lo, core), col: 8 (over y, x_hi).
Axes of the slice: x: 4 (x_hi: 2, x_lo: 2; x = x_hi * 2 + x_lo), y: 4, z: 8, core: 2. Of those that a mesh axis runs over, the one named last changes fastest.
Arguments:
- vectors: bfloat16 [8, 262144], P(None, ('row', 'col')), may hold values from -6 to 6
- energies: float32 [262144], P(('row', 'col')), may hold values from 0.5 to 6
- tiles: bfloat16 [262144, 4096], P(('row', 'col')), may hold values from -0.25 to 0.25
- tile_rows: int32 [262144], P(('row', 'col')), may hold values from 0 to 127, as said below
- tile_cols: int32 [262144], P(('row', 'col')), may hold values from 0 to 511
- tile_count: int32 [256], P(('row', 'col')), may hold values from 128 to 1024, as said below
Outputs:
- product: bfloat16 [8, 262144], P(None, ('row', 'col'))
- residual: float32 [8, 262144], P(None, ('row', 'col'))
Inputs may be any that keep to these rules, and one draw needn't show every extreme that they name: `tile_count`: every count is at least 128, and some device uses all 1024 slots in every draw; a few devices are full while most use far fewer. `tile_rows`: slots may name the same row and column block more than once; such tiles add.
All inputs are finite; a program needn't handle non-finite values.
Results may differ from a plain program's by a relative error of at most 0.008.
Values may be sent and summed in bfloat16 or wider, within the bound.
A program may use at most 64 MiB of HBM per device.

v0:
```python
import jax
import jax.numpy as jnp
from jax import lax
from jax.sharding import PartitionSpec as P


def per_device(vectors, energies, tiles, tile_rows, tile_cols, tile_count):
    kvec = vectors.shape[0]
    own_states = vectors.shape[1]
    blk_own = own_states // 64
    n_row = lax.axis_size("row")
    n_col = lax.axis_size("col")
    seg_blocks = n_col * blk_own
    slots = tiles.shape[0]
    group = min(128, slots)
    gathered = lax.all_gather(vectors, "row", axis=1, tiled=True)
    blocks = gathered.reshape(kvec, n_row * blk_own, 64)
    seg_ids = jnp.arange(seg_blocks, dtype=jnp.int32)
    group_ids = jnp.arange(group, dtype=jnp.int32)
    count = tile_count[0]
    turns = (count + group - 1) // group

    def add_group(step, accum):
        first = step * group
        tile_part = lax.dynamic_slice_in_dim(tiles, first, group, 0).reshape(group, 64, 64)
        row_part = lax.dynamic_slice_in_dim(tile_rows, first, group, 0)
        col_part = lax.dynamic_slice_in_dim(tile_cols, first, group, 0)
        picked = jnp.take(blocks, col_part, axis=1)
        prod = jnp.einsum("tji,kti->ktj", tile_part, picked, preferred_element_type=jnp.float32)
        live = first + group_ids < count
        onehot = ((row_part[:, None] == seg_ids[None, :]) & live[:, None]).astype(jnp.bfloat16)
        upper = prod.astype(jnp.bfloat16)
        lower = (prod - upper.astype(jnp.float32)).astype(jnp.bfloat16)
        added = jnp.einsum("ktj,tr->krj", upper, onehot, preferred_element_type=jnp.float32)
        added = added + jnp.einsum("ktj,tr->krj", lower, onehot, preferred_element_type=jnp.float32)
        return accum + added

    accum = jnp.zeros((kvec, seg_blocks, 64), jnp.float32)
    accum = lax.fori_loop(0, turns, add_group, accum)
    partial_value = accum.reshape(kvec, seg_blocks * 64)
    summed = lax.psum(partial_value.astype(jnp.bfloat16), "col").astype(jnp.float32)
    share = lax.dynamic_slice_in_dim(summed, lax.axis_index("col") * own_states, own_states, 1)
    vec32 = vectors.astype(jnp.float32)
    diag_part = energies[None, :] * vec32
    whole = diag_part + share
    terms = jnp.einsum("an,bn->ab", vec32, whole, precision=lax.Precision.HIGHEST)
    total_states = n_row * n_col * own_states
    gram = lax.psum(terms, ("row", "col")) / total_states
    residual = whole - jnp.einsum("ab,an->bn", gram, vec32, precision=lax.Precision.HIGHEST)
    return (whole.astype(jnp.bfloat16), residual)


def solution(mesh):
    in_specs = (
        P(None, ("row", "col")),
        P(("row", "col")),
        P(("row", "col"), None),
        P(("row", "col")),
        P(("row", "col")),
        P(("row", "col")),
    )
    out_specs = (P(None, ("row", "col")), P(None, ("row", "col")))
    return jax.shard_map(
        per_device, mesh=mesh, in_specs=in_specs, out_specs=out_specs, check_vma=False
    )
```

profile of v0, /device:TPU:1, one launch (start us, length us, event | category | flops | bytes accessed | tf_op | source)
XLA Modules:
  0.0 307.5 jit_solution(10586212366115992367)
XLA Ops:
  7.2 0.0 all-reduce.2.cloned.1.call-start
  7.9 40.2 %all_gather.3 = bf16[8,32768]{1,0:T(8,128)(2,1)S(1)} all-gather(bf16[8,1024]{1,0:T(8,128)(2,1)} %param.8), channel_id=1, replica_groups=mesh['row'=32,'col'=8] {'row'}, dimensions={1}, use_global_device_ids=true | all-gather | bytes 540672 | tf_op jit(solution)/shard_map/all_gather | solution.py:16
  48.0 1.1 reshape.25
  49.2 1.7 copy.20
  50.8 0.0 copy-start
  50.9 0.0 copy-start.1
  50.9 22.4 %while.13 = (s32[]{:T(128)}, f32[8,128,64]{1,2,0:T(8,128)S(1)}, s32[]{:T(128)}, s32[1024]{0:T(1024)}, s32[]{:T(128)}, /*index=5*/s32[1024]{0:T(1024)}, bf16[8,51...) while((s32[]{:T(128)}, f32[8,128,64]{1,2,0:T(8,128)S(1)}, ...), condition=%wide.region_1.2_spmd.clone.clone, body=%wide.region_0.1_spmd.clone.clone.sunk | while | flops 42469380 | bytes 10887999 | solution.py:39
  50.9 1.3 constant_dynamic-slice_fusion.2
  52.2 0.7 copy.27
  52.9 2.9 copy.28
  55.8 1.4 compare_and_fusion.2
  57.2 1.9 gather_fusion
  59.1 1.2 fusion.47
  60.4 0.2 copy.29
  60.6 0.1 fusion.48
  60.7 0.8 dynamic_slice.35
  61.4 0.3 fusion.49
  61.7 0.3 fusion.50
  62.0 0.1 bitcast_add_fusion.2
  62.1 1.3 constant_dynamic-slice_fusion.2
  63.4 0.7 copy.27
  64.1 2.9 copy.28
  67.0 1.4 compare_and_fusion.2
  68.4 1.9 gather_fusion
  70.3 1.2 fusion.47
  71.6 0.2 copy.29
  71.8 0.1 fusion.48
  71.9 0.8 dynamic_slice.35
  72.6 0.3 fusion.49
  72.9 0.3 fusion.50
  73.2 0.1 bitcast_add_fusion.2
  73.3 0.2 copy.22
  73.5 0.9 convert_element_type.31
  74.4 0.0 all-reduce.2.cloned.1.call-update
  74.5 143.2 %all-reduce.2.cloned.1.call-done = bf16[8,8192]{1,0:T(8,128)(2,1)} async-done(((bf16[8,8192]{1,0:T(8,128)(2,1)}), bf16[8,8192]{1,0:T(8,128)(2,1)}) %all-reduce.2.cloned.1.call-update) | async-done | bytes 131088 | tf_op jit(solution)/shard_map/psum | solution.py:41
  217.7 0.0 copy-done
  217.7 0.0 copy-done.1
  217.7 0.8 convolution_bitcast_fusion
  218.5 79.3 %psum.15 = f32[8,8]{0,1:T(8,128)S(1)} all-reduce(f32[8,8]{0,1:T(8,128)S(1)} %convolution_bitcast_fusion), channel_id=1, replica_groups=mesh['row'=32,'col'=8] {'row','col'}, use_global_device_ids=true, to_apply=%region_3.4 | all-reduce | flops 64 | bytes 512 | tf_op jit(solution)/shard_map/psum | solution.py:48
  297.8 1.3 fusion.19
  299.2 1.5 convolution_subtract_fusion
  (4 shorter events, 0.0 us)
Async XLA Ops:
  7.2 210.5 %all-reduce.2.cloned.1.call-start = ((), (), s32[]{:S(2)}) async-start(), calls=%async_computation | async-start | bytes 262144 | tf_op jit(solution)/shard_map/psum | solution.py:41
  50.8 166.9 %copy-start = (bf16[8,1024]{1,0:T(8,128)(2,1)S(1)}, bf16[8,1024]{1,0:T(8,128)(2,1)}, u32[]{:S(2)}) copy-start(bf16[8,1024]{1,0:T(8,128)(2,1)} %param.8) | copy-start | bytes 49156
  50.9 166.9 %copy-start.1 = (f32[1024]{0:T(1024)S(1)}, f32[1024]{0:T(1024)}, u32[]{:S(2)}) copy-start(f32[1024]{0:T(1024)} %param.9) | copy-start | bytes 12292
Sparse Core Ops, SparseCore 0:
  74.6 143.0 all-reduce.1
where the time goes:
time: 309 us; the launch traced here: 307 us
  waiting for transfers between devices  143 us (46%)
  blocking collectives  119 us (39%)
  local copies, waits for them, and re-layouts  19.5 us (6%)
  between operations  14.7 us (5%)
  matrix products  5.8 us (2%)
  other arithmetic  4.52 us (1%)
    psum x1, waiting for transfers between devices, per_device(): lax.psum(partial_value.astype(jnp.bfloat16), 'col').astype(jnp.float32)  143 us
    psum x1, blocking collectives, per_device(): gram = lax.psum(terms, ('row', 'col')) / total_states  79.3 us
    all_gather x1, blocking collectives, per_device(): gathered = lax.all_gather(vectors, 'row', axis=1, tiled=True)  40.2 us
  transfers between devices with their start and end apart: 1, of which 1 were waited for; matrix products, arithmetic and copies ran while one was open for 0% of the time, Pallas kernels for 0%

commit v1 on v0

--- a/solution.py
+++ b/solution.py
@@ -45,7 +45,12 @@
     whole = diag_part + share
     terms = jnp.einsum("an,bn->ab", vec32, whole, precision=lax.Precision.HIGHEST)
     total_states = n_row * n_col * own_states
-    gram = lax.psum(terms, ("row", "col")) / total_states
+
+    def lay_stages_all(arr_in, a_name):
+        last = lax.all_gather(arr_in, a_name).sum(axis=0)
+        return last
+
+    gram = lay_stages_all(terms, ("row", "col")) / total_states
     residual = whole - jnp.einsum("ab,an->bn", gram, vec32, precision=lax.Precision.HIGHEST)
     return (whole.astype(jnp.bfloat16), residual)
 

time: 309 us -> 860 us (2.78); the launches traced: 307 us -> 849 us
  blocking collectives: 119 us -> 661 us
    all_gather x0 -> x1, blocking collectives: none -> 621 us  [lay_stages_all(): last = lax.all_gather(arr_in, a_name).sum(axis=0)]
    psum x1 -> x0, blocking collectives: 79.3 us -> none  [per_device(): gram = lax.psum(terms, ('row', 'col')) / total_states]
where the time goes in v1:
time: 860 us; the launch traced here: 849 us
  blocking collectives  661 us (77%)
  waiting for transfers between devices  143 us (17%)
  local copies, waits for them, and re-layouts  19.7 us (2%)
  between operations  14.7 us (2%)
    all_gather x1, blocking collectives, lay_stages_all(): last = lax.all_gather(arr_in, a_name).sum(axis=0)  621 us
    psum x1, waiting for transfers between devices, per_device(): lax.psum(partial_value.astype(jnp.bfloat16), 'col').astype(jnp.float32)  143 us
    all_gather x1, blocking collectives, per_device(): gathered = lax.all_gather(vectors, 'row', axis=1, tiled=True)  40.2 us
  transfers between devices with their start and end apart: 1, of which 1 were waited for; matrix products, arithmetic and copies ran while one was open for 0% of the time, Pallas kernels for 0%

profile of v1, /device:TPU:1, one launch (start us, length us, event | category | flops | bytes accessed | tf_op | source)
XLA Modules:
  0.0 849.3 jit_solution(17125459617874427160)
XLA Ops:
  7.2 0.0 all-reduce.2.cloned.1.call-start
  7.9 40.2 %all_gather.9 = bf16[8,32768]{1,0:T(8,128)(2,1)S(1)} all-gather(bf16[8,1024]{1,0:T(8,128)(2,1)} %param.8), channel_id=1, replica_groups=mesh['row'=32,'col'=8] {'row'}, dimensions={1}, use_global_device_ids=true | all-gather | bytes 540672 | tf_op jit(solution)/shard_map/all_gather | solution.py:16
  48.0 1.1 reshape.25
  49.2 1.7 copy.28
  50.8 0.0 copy-start
  50.9 0.0 copy-start.1
  50.9 22.4 %while.13 = (s32[]{:T(128)}, f32[8,128,64]{1,2,0:T(8,128)S(1)}, s32[]{:T(128)}, s32[1024]{0:T(1024)}, s32[]{:T(128)}, /*index=5*/s32[1024]{0:T(1024)}, bf16[8,51...) while((s32[]{:T(128)}, f32[8,128,64]{1,2,0:T(8,128)S(1)}, ...), condition=%wide.region_1.2_spmd.clone.clone, body=%wide.region_0.1_spmd.clone.clone.sunk | while | flops 42469380 | bytes 10887999 | solution.py:39
  50.9 1.3 constant_dynamic-slice_fusion.2
  52.2 0.7 copy.39
  52.9 2.9 copy.40
  55.8 1.4 compare_and_fusion.2
  57.2 1.9 gather_fusion
  59.1 1.2 fusion.47
  60.4 0.2 copy.41
  60.6 0.1 fusion.48
  60.7 0.8 dynamic_slice.35
  61.4 0.3 fusion.49
  61.7 0.3 fusion.50
  62.0 0.1 bitcast_add_fusion.2
  62.1 1.3 constant_dynamic-slice_fusion.2
  63.4 0.7 copy.39
  64.1 2.9 copy.40
  67.0 1.4 compare_and_fusion.2
  68.4 1.9 gather_fusion
  70.3 1.2 fusion.47
  71.6 0.2 copy.41
  71.8 0.1 fusion.48
  71.9 0.8 dynamic_slice.35
  72.6 0.3 fusion.49
  72.9 0.3 fusion.50
  73.2 0.1 bitcast_add_fusion.2
  73.3 0.2 copy.30
  73.5 0.9 convert_element_type.31
  74.4 0.0 all-reduce.2.cloned.1.call-update
  74.5 143.2 %all-reduce.2.cloned.1.call-done = bf16[8,8192]{1,0:T(8,128)(2,1)} async-done(((bf16[8,8192]{1,0:T(8,128)(2,1)}), bf16[8,8192]{1,0:T(8,128)(2,1)}) %all-reduce.2.cloned.1.call-update) | async-done | bytes 131088 | tf_op jit(solution)/shard_map/psum | solution.py:41
  217.7 0.0 copy-done
  217.7 0.0 copy-done.1
  217.7 0.8 convolution_bitcast_fusion
  218.5 0.1 copy.31
  218.6 620.7 %all-gather = f32[2048,8]{1,0:T(8,128)S(1)} all-gather(f32[8,8]{1,0:T(8,128)S(1)} %copy.31), channel_id=2, replica_groups=mesh['row'=32,'col'=8] {'row','col'}, dimensions={0}, use_global_device_ids=true | all-gather | bytes 65792 | tf_op jit(solution)/shard_map/all_gather | solution.py:50
  839.3 0.3 bitcast_reduce_fusion
  839.6 0.1 copy.35
  839.7 1.3 fusion.19
  841.0 1.5 convolution_subtract_fusion
  (4 shorter events, 0.0 us)
Async XLA Ops:
  7.2 210.5 %all-reduce.2.cloned.1.call-start = ((), (), s32[]{:S(2)}) async-start(), calls=%async_computation | async-start | bytes 262144 | tf_op jit(solution)/shard_map/psum | solution.py:41
  50.8 166.9 %copy-start = (bf16[8,1024]{1,0:T(8,128)(2,1)S(1)}, bf16[8,1024]{1,0:T(8,128)(2,1)}, u32[]{:S(2)}) copy-start(bf16[8,1024]{1,0:T(8,128)(2,1)} %param.8) | copy-start | bytes 49156
  50.9 166.9 %copy-start.1 = (f32[1024]{0:T(1024)S(1)}, f32[1024]{0:T(1024)}, u32[]{:S(2)}) copy-start(f32[1024]{0:T(1024)} %param.9) | copy-start | bytes 12292
Sparse Core Ops, SparseCore 0:
  74.6 143.0 all-reduce.1
